TPU v7x, 32 devices: a whole 2x2x4 slice. The times are simulated.
32 devices in a mesh: cand: 4 (over x, core), seq: 8 (over z, y).
Axes of the slice: x: 2, y: 2, z: 4, core: 2. Of those that a mesh axis runs over, the one named last changes fastest.
Arguments:
- response_query_array: bfloat16 [8, 768, 2560], P('cand', 'seq'), may hold values from -180 to 180
- response_key_array: bfloat16 [8, 768, 512], P('cand', 'seq'), may hold values from -6 to 6
- response_value_array: bfloat16 [8, 768, 512], P('cand', 'seq'), may hold values from -6 to 6
- prompt_key_array: bfloat16 [2048, 512], P(('cand', 'seq')), may hold values from -6 to 6
- prompt_value_array: bfloat16 [2048, 512], P(('cand', 'seq')), may hold values from -6 to 6
- lengths: int32 [8], replicated, may hold values from 192 to 768, as said below
- offsets: int32 [8], replicated, may hold values from 512 to 2048, as said below
- ranks: int32 [8], replicated, may hold values from 0 to 7, each once
Outputs:
- attention: bfloat16 [8, 768, 2560], P('cand', 'seq')
Inputs may be any that keep to these rules, and one draw needn't show every extreme that they name: `lengths`: some candidate's response has all 768 positions live. `offsets`: some candidate sees the whole prompt.
All inputs are finite; a program needn't handle non-finite values.
Results may differ from a plain program's by a relative error of at most 0.004.
Values may be sent and summed in bfloat16 or wider, within the bound.
No kernel may reach another device: no remote copies, remote signals or barrier semaphores. Data moves between devices by JAX's collectives and lax.ppermute only.
A program may use at most 128 MiB of HBM per device.

v0:
```python
import math
import jax
import jax.numpy as jnp
from jax import lax
from jax.sharding import PartitionSpec as P

QUERY_HEADS = 20
KEY_VALUE_HEADS = 4
HEAD_DIMENSION = 128
lowest_score_value = -1e30


def attend_block(running, query_rows, block_keys, block_values, allowed, shared):
    running_max, running_total, running_sum = running
    cand_count = query_rows.shape[0]
    heads_kv = query_rows.shape[2]
    head_size = query_rows.shape[4]
    score_scale = 1.0 / math.sqrt(head_size)
    if shared:
        keys_split = block_keys.reshape(block_keys.shape[0], heads_kv, head_size)
        values_split = block_values.reshape(block_values.shape[0], heads_kv, head_size)
        scores = jnp.einsum(
            "crhgd,nhd->chgrn", query_rows, keys_split, preferred_element_type=jnp.float32
        )
    else:
        keys_split = block_keys.reshape(cand_count, block_keys.shape[1], heads_kv, head_size)
        values_split = block_values.reshape(cand_count, block_values.shape[1], heads_kv, head_size)
        scores = jnp.einsum(
            "crhgd,cnhd->chgrn", query_rows, keys_split, preferred_element_type=jnp.float32
        )
    scores = jnp.where(allowed[:, None, None, :, :], scores * score_scale, -jnp.inf)
    new_max = jnp.maximum(running_max, jnp.max(scores, axis=-1))
    rescale = jnp.exp(running_max - new_max)
    exponent = jnp.exp(scores - new_max[..., None])
    weights = exponent.astype(jnp.bfloat16)
    new_total = running_total * rescale + jnp.sum(exponent, axis=-1)
    if shared:
        contrib = jnp.einsum(
            "chgrn,nhd->chgrd", weights, values_split, preferred_element_type=jnp.float32
        )
    else:
        contrib = jnp.einsum(
            "chgrn,cnhd->chgrd", weights, values_split, preferred_element_type=jnp.float32
        )
    new_sum = running_sum * rescale[..., None] + contrib
    return (new_max, new_total, new_sum)


def fold_blocks(
    running, query_rows, all_keys, all_values, key_pos, allowed_of, shared, live_of=None
):
    key_count = key_pos.shape[0]
    block_len = math.gcd(key_count, 512)
    keys_axis = 0 if shared else 1

    def one_block(step_at, carried):
        block_start = step_at * block_len
        block_keys = lax.dynamic_slice_in_dim(all_keys, block_start, block_len, keys_axis)
        block_values = lax.dynamic_slice_in_dim(all_values, block_start, block_len, keys_axis)
        block_pos = lax.dynamic_slice_in_dim(key_pos, block_start, block_len, 0)
        return attend_block(
            carried, query_rows, block_keys, block_values, allowed_of(block_pos), shared
        )

    return lax.fori_loop(0, key_count // block_len, one_block, running)


def body(
    response_query_array,
    response_key_array,
    response_value_array,
    prompt_key_array,
    prompt_value_array,
    lengths,
    offsets,
    ranks,
):
    candidate_local, output_rows, width = response_query_array.shape
    group_width = QUERY_HEADS // KEY_VALUE_HEADS
    group_at = lax.axis_index("cand")
    seq_at = lax.axis_index("seq")
    first_cand = group_at * candidate_local
    my_lengths = lax.dynamic_slice_in_dim(lengths, first_cand, candidate_local)
    my_offsets = lax.dynamic_slice_in_dim(offsets, first_cand, candidate_local)
    query_pos = seq_at * output_rows + jnp.arange(output_rows, dtype=jnp.int32)
    query_rows = response_query_array.reshape(
        candidate_local, output_rows, KEY_VALUE_HEADS, group_width, HEAD_DIMENSION
    )
    pieces = (
        lax.all_gather(prompt_key_array, ("cand", "seq"), axis=0, tiled=True),
        lax.all_gather(prompt_value_array, ("cand", "seq"), axis=0, tiled=True),
    )
    key_pos = jnp.arange(pieces[0].shape[0], dtype=jnp.int32)

    def allowed_of(block_pos):
        return block_pos[None, None, :] < my_offsets[:, None, None]

    running = fold_blocks(
        (
            jnp.full(
                (candidate_local, KEY_VALUE_HEADS, group_width, output_rows),
                lowest_score_value,
                jnp.float32,
            ),
            jnp.zeros((candidate_local, KEY_VALUE_HEADS, group_width, output_rows), jnp.float32),
            jnp.zeros(
                (candidate_local, KEY_VALUE_HEADS, group_width, output_rows, HEAD_DIMENSION),
                jnp.float32,
            ),
        ),
        query_rows,
        pieces[0],
        pieces[1],
        key_pos,
        allowed_of,
        True,
    )
    pieces = (
        lax.all_gather(response_key_array, "seq", axis=1, tiled=True),
        lax.all_gather(response_value_array, "seq", axis=1, tiled=True),
    )
    key_pos = jnp.arange(pieces[0].shape[1], dtype=jnp.int32)

    def allowed_of(block_pos):
        causal = block_pos[None, None, :] <= query_pos[None, :, None]
        return causal & (block_pos[None, None, :] < my_lengths[:, None, None])

    final_max, final_total, final_sum = fold_blocks(
        running, query_rows, pieces[0], pieces[1], key_pos, allowed_of, False
    )
    attended = final_sum / final_total[..., None]
    attended = jnp.transpose(attended, (0, 3, 1, 2, 4)).reshape(candidate_local, output_rows, width)
    row_valid = query_pos[None, :] < my_lengths[:, None]
    attended = jnp.where(row_valid[:, :, None], attended, 0.0).astype(jnp.bfloat16)
    gathered = lax.all_gather(attended, "cand", axis=0, tiled=True)
    every_cand = jnp.arange(gathered.shape[0], dtype=jnp.int32)
    chosen = []
    for within in range(candidate_local):
        target = first_cand + within
        source = jnp.sum(jnp.where(ranks == target, every_cand, 0))
        chosen.append(lax.dynamic_index_in_dim(gathered, source, 0, keepdims=False))
    return jnp.stack(chosen, axis=0)


def solution(mesh):
    in_specs = (
        P("cand", "seq", None),
        P("cand", "seq", None),
        P("cand", "seq", None),
        P(("cand", "seq"), None),
        P(("cand", "seq"), None),
        P(),
        P(),
        P(),
    )
    out_specs = P("cand", "seq", None)
    return jax.shard_map(body, mesh=mesh, in_specs=in_specs, out_specs=out_specs, check_vma=False)
```

profile of v0, /device:TPU:0, one launch (start us, length us, event | category | flops | bytes accessed | tf_op | source)
XLA Modules:
  0.0 304.9 jit_solution(10088347945177968936)
XLA Ops:
  8.1 1.8 copy.56
  9.9 1.8 copy.57
  15.9 53.7 %all-gather.6.cloned.1.call-done = bf16[2048,512]{1,0:T(8,128)(2,1)} async-done(((bf16[64,512]{1,0:T(8,128)(2,1)}), bf16[2048,512]{1,0:T(8,128)(2,1)}) %all-gather.6.cloned.1.call-update) | async-done | bytes 2097168 | tf_op jit(solution)/shard_map/all_gather | solution.py:90
  69.6 58.4 %all-gather.8.cloned.1.call-done = bf16[2048,512]{1,0:T(8,128)(2,1)} async-done(((bf16[64,512]{1,0:T(8,128)(2,1)}), bf16[2048,512]{1,0:T(8,128)(2,1)}) %all-gather.8.cloned.1.call-update) | async-done | bytes 2097168 | tf_op jit(solution)/shard_map/all_gather | solution.py:91
  128.0 65.4 %while.37 = (s32[]{:T(128)}, f32[2,4,5,96]{3,2,0,1:T(8,128)S(1)}, f32[2,4,5,96]{3,2,0,1:T(8,128)S(1)}, f32[2,4,5,96,128]{4,3,2,0,1:T(8,128)}, s32[2048]{0:T(1024...) while((s32[]{:T(128)}, f32[2,4,5,96]{3,2,0,1:T(8,128)S(1)}, ...), condition=%wide.region_3.4_spmd.clone, body=%wide.region_0.3_spmd.clone.sunk | while | flops 1029754624 | bytes 34007236 | solution.py:65
  129.6 4.2 %fusion.60 = (f32[2,4,5,96]{3,2,0,1:T(8,128)S(1)}, f32[4,512,2,96,5]{1,3,4,2,0:T(8,128)}) fusion(pred[2,512]{1,0:T(4,128)(4,1)S(1)} %broadcast_compare_fusion.9, bf16[512,4,128,1,1]{0,2,4,3,1:T(8,128)(2,1)S(1)} %bitcast.88, bf16[2,96,4,5,128]{4,1,3,0,2:T(8,128)(2,1)S(1)} %get-tuple-element.683), kind=kOutput, calls=%fused_computation.26.clone.1 | convolution fusion | flops 509210880 | bytes 9388032 | tf_op jit(solution)/shard_map/while/body/eval_jaxpr/crhgd,nhd->chgrn/dot_general | solution.py:22
  133.9 4.5 %fusion.61 = f32[2,4,5,96]{3,2,0,1:T(8,128)S(1)} fusion(f32[4,512,2,96,5]{1,3,4,2,0:T(8,128)} %get-tuple-element.646, f32[2,4,5,96]{3,2,0,1:T(8,128)S(1)} %select_maximum_fusion.2, pred[2,512]{1,0:T(4,128)(4,1)S(1)} %broadcast_compare_fusion.9), kind=kLoop, calls=%fused_computation.25.clone.1 | loop fusion | flops 7860480 | bytes 7896064 | tf_op jit(solution)/shard_map/while/body/eval_jaxpr/reduce_sum | solution.py:36
  138.6 5.4 %bitcast_add_fusion.2 = f32[2,4,5,96,128]{4,3,2,0,1:T(8,128)} fusion(f32[2,4,5,96,128]{4,3,2,0,1:T(8,128)} %get-tuple-element.666, bf16[512,4,128,1,1]{0,2,4,3,1:T(8,128)(2,1)S(1)} %bitcast.91, f32[4,512,2,96,5]{1,3,4,2,0:T(8,128)} %get-tuple-element.646, f32[2,4,5,96]{3,2,0,1:T(8,128)S(1)} %select_maximum_fusion.2, ...), kind=kOutput, calls=%fused_computation.32.clone.1 | convolution fusion | flops 512655360 | bytes 12352513 | tf_op jit(solution)/shard_map/while/body/eval_jaxpr/chgrn,nhd->chgrd/dot_general | solution.py:38
  145.7 4.2 %fusion.60 = (f32[2,4,5,96]{3,2,0,1:T(8,128)S(1)}, f32[4,512,2,96,5]{1,3,4,2,0:T(8,128)}) fusion(pred[2,512]{1,0:T(4,128)(4,1)S(1)} %broadcast_compare_fusion.9, bf16[512,4,128,1,1]{0,2,4,3,1:T(8,128)(2,1)S(1)} %bitcast.88, bf16[2,96,4,5,128]{4,1,3,0,2:T(8,128)(2,1)S(1)} %get-tuple-element.683), kind=kOutput, calls=%fused_computation.26.clone.1 | convolution fusion | flops 509210880 | bytes 9388032 | tf_op jit(solution)/shard_map/while/body/eval_jaxpr/crhgd,nhd->chgrn/dot_general | solution.py:22
  149.9 4.4 %fusion.61 = f32[2,4,5,96]{3,2,0,1:T(8,128)S(1)} fusion(f32[4,512,2,96,5]{1,3,4,2,0:T(8,128)} %get-tuple-element.646, f32[2,4,5,96]{3,2,0,1:T(8,128)S(1)} %select_maximum_fusion.2, pred[2,512]{1,0:T(4,128)(4,1)S(1)} %broadcast_compare_fusion.9), kind=kLoop, calls=%fused_computation.25.clone.1 | loop fusion | flops 7860480 | bytes 7896064 | tf_op jit(solution)/shard_map/while/body/eval_jaxpr/reduce_sum | solution.py:36
  154.6 6.0 %bitcast_add_fusion.2 = f32[2,4,5,96,128]{4,3,2,0,1:T(8,128)} fusion(f32[2,4,5,96,128]{4,3,2,0,1:T(8,128)} %get-tuple-element.666, bf16[512,4,128,1,1]{0,2,4,3,1:T(8,128)(2,1)S(1)} %bitcast.91, f32[4,512,2,96,5]{1,3,4,2,0:T(8,128)} %get-tuple-element.646, f32[2,4,5,96]{3,2,0,1:T(8,128)S(1)} %select_maximum_fusion.2, ...), kind=kOutput, calls=%fused_computation.32.clone.1 | convolution fusion | flops 512655360 | bytes 12352513 | tf_op jit(solution)/shard_map/while/body/eval_jaxpr/chgrn,nhd->chgrd/dot_general | solution.py:38
  162.2 4.2 %fusion.60 = (f32[2,4,5,96]{3,2,0,1:T(8,128)S(1)}, f32[4,512,2,96,5]{1,3,4,2,0:T(8,128)}) fusion(pred[2,512]{1,0:T(4,128)(4,1)S(1)} %broadcast_compare_fusion.9, bf16[512,4,128,1,1]{0,2,4,3,1:T(8,128)(2,1)S(1)} %bitcast.88, bf16[2,96,4,5,128]{4,1,3,0,2:T(8,128)(2,1)S(1)} %get-tuple-element.683), kind=kOutput, calls=%fused_computation.26.clone.1 | convolution fusion | flops 509210880 | bytes 9388032 | tf_op jit(solution)/shard_map/while/body/eval_jaxpr/crhgd,nhd->chgrn/dot_general | solution.py:22
  166.4 4.4 %fusion.61 = f32[2,4,5,96]{3,2,0,1:T(8,128)S(1)} fusion(f32[4,512,2,96,5]{1,3,4,2,0:T(8,128)} %get-tuple-element.646, f32[2,4,5,96]{3,2,0,1:T(8,128)S(1)} %select_maximum_fusion.2, pred[2,512]{1,0:T(4,128)(4,1)S(1)} %broadcast_compare_fusion.9), kind=kLoop, calls=%fused_computation.25.clone.1 | loop fusion | flops 7860480 | bytes 7896064 | tf_op jit(solution)/shard_map/while/body/eval_jaxpr/reduce_sum | solution.py:36
  171.1 5.9 %bitcast_add_fusion.2 = f32[2,4,5,96,128]{4,3,2,0,1:T(8,128)} fusion(f32[2,4,5,96,128]{4,3,2,0,1:T(8,128)} %get-tuple-element.666, bf16[512,4,128,1,1]{0,2,4,3,1:T(8,128)(2,1)S(1)} %bitcast.91, f32[4,512,2,96,5]{1,3,4,2,0:T(8,128)} %get-tuple-element.646, f32[2,4,5,96]{3,2,0,1:T(8,128)S(1)} %select_maximum_fusion.2, ...), kind=kOutput, calls=%fused_computation.32.clone.1 | convolution fusion | flops 512655360 | bytes 12352513 | tf_op jit(solution)/shard_map/while/body/eval_jaxpr/chgrn,nhd->chgrd/dot_general | solution.py:38
  178.6 4.2 %fusion.60 = (f32[2,4,5,96]{3,2,0,1:T(8,128)S(1)}, f32[4,512,2,96,5]{1,3,4,2,0:T(8,128)}) fusion(pred[2,512]{1,0:T(4,128)(4,1)S(1)} %broadcast_compare_fusion.9, bf16[512,4,128,1,1]{0,2,4,3,1:T(8,128)(2,1)S(1)} %bitcast.88, bf16[2,96,4,5,128]{4,1,3,0,2:T(8,128)(2,1)S(1)} %get-tuple-element.683), kind=kOutput, calls=%fused_computation.26.clone.1 | convolution fusion | flops 509210880 | bytes 9388032 | tf_op jit(solution)/shard_map/while/body/eval_jaxpr/crhgd,nhd->chgrn/dot_general | solution.py:22
  182.8 4.4 %fusion.61 = f32[2,4,5,96]{3,2,0,1:T(8,128)S(1)} fusion(f32[4,512,2,96,5]{1,3,4,2,0:T(8,128)} %get-tuple-element.646, f32[2,4,5,96]{3,2,0,1:T(8,128)S(1)} %select_maximum_fusion.2, pred[2,512]{1,0:T(4,128)(4,1)S(1)} %broadcast_compare_fusion.9), kind=kLoop, calls=%fused_computation.25.clone.1 | loop fusion | flops 7860480 | bytes 7896064 | tf_op jit(solution)/shard_map/while/body/eval_jaxpr/reduce_sum | solution.py:36
  187.5 5.9 %bitcast_add_fusion.2 = f32[2,4,5,96,128]{4,3,2,0,1:T(8,128)} fusion(f32[2,4,5,96,128]{4,3,2,0,1:T(8,128)} %get-tuple-element.666, bf16[512,4,128,1,1]{0,2,4,3,1:T(8,128)(2,1)S(1)} %bitcast.91, f32[4,512,2,96,5]{1,3,4,2,0:T(8,128)} %get-tuple-element.646, f32[2,4,5,96]{3,2,0,1:T(8,128)S(1)} %select_maximum_fusion.2, ...), kind=kOutput, calls=%fused_computation.32.clone.1 | convolution fusion | flops 512655360 | bytes 12352513 | tf_op jit(solution)/shard_map/while/body/eval_jaxpr/chgrn,nhd->chgrd/dot_general | solution.py:38
  196.3 22.1 %all-gather.12.cloned.1.call-done = bf16[2,768,512]{2,0,1:T(2,128)(2,1)} async-done(((bf16[2,96,512]{2,0,1:T(2,128)(2,1)}), bf16[2,768,512]{2,0,1:T(2,128)(2,1)}) %all-gather.12.cloned.1.call-update) | async-done | bytes 1572880 | tf_op jit(solution)/shard_map/all_gather | solution.py:120
  218.4 41.8 %while.36 = (s32[]{:T(128)}, f32[2,4,5,96]{3,2,1,0:T(8,128)}, f32[2,4,5,96]{3,2,1,0:T(8,128)}, f32[2,4,5,96,128]{4,3,2,1,0:T(8,128)S(1)}, s32[768]{0:T(1024)S(1)...) while((s32[]{:T(128)}, f32[2,4,5,96]{3,2,1,0:T(8,128)}, ...), condition=%wide.region_7.8_spmd.clone, body=%wide.region_4.7_spmd.clone.sunk | while | flops 515194976 | bytes 38561872 | solution.py:65
  219.3 1.9 constant_dynamic-slice_fusion.8
  221.8 2.2 fusion.54
  224.0 1.8 copy-done
  228.0 3.7 %multiply_add_fusion.5 = f32[2,4,5,96,128]{4,3,2,1,0:T(8,128)S(1)} fusion(f32[2,4,5,96,128]{4,3,2,1,0:T(8,128)S(1)} %get-tuple-element.706, bf16[2,256,4,128,1]{1,3,4,2,0:T(8,128)(2,1)S(1)} %bitcast.89, f32[2,4,256,96,5]{2,3,4,1,0:T(8,128)} %copy-done, f32[2,4,5,96]{3,2,1,0:T(8,128)S(1)} %max.19, pred[2,96,256]{2,1,0:T(8,128)(4,1)S(1)} %copy-done.1, ...), kind=kOutput, calls=%fused_computation.7.clone.1 | convolution fusion | flops 256573440 | bytes 8468480 | tf_op jit(solution)/shard_map/while/body/eval_jaxpr/chgrn,cnhd->chgrd/dot_general | solution.py:42
  233.2 1.9 constant_dynamic-slice_fusion.8
  235.7 2.2 fusion.54
  238.0 1.8 copy-done
  241.9 3.7 %multiply_add_fusion.5 = f32[2,4,5,96,128]{4,3,2,1,0:T(8,128)S(1)} fusion(f32[2,4,5,96,128]{4,3,2,1,0:T(8,128)S(1)} %get-tuple-element.706, bf16[2,256,4,128,1]{1,3,4,2,0:T(8,128)(2,1)S(1)} %bitcast.89, f32[2,4,256,96,5]{2,3,4,1,0:T(8,128)} %copy-done, f32[2,4,5,96]{3,2,1,0:T(8,128)S(1)} %max.19, pred[2,96,256]{2,1,0:T(8,128)(4,1)S(1)} %copy-done.1, ...), kind=kOutput, calls=%fused_computation.7.clone.1 | convolution fusion | flops 256573440 | bytes 8468480 | tf_op jit(solution)/shard_map/while/body/eval_jaxpr/chgrn,cnhd->chgrd/dot_general | solution.py:42
  247.2 1.9 constant_dynamic-slice_fusion.8
  249.7 2.2 fusion.54
  251.9 1.8 copy-done
  255.9 3.7 %multiply_add_fusion.5 = f32[2,4,5,96,128]{4,3,2,1,0:T(8,128)S(1)} fusion(f32[2,4,5,96,128]{4,3,2,1,0:T(8,128)S(1)} %get-tuple-element.706, bf16[2,256,4,128,1]{1,3,4,2,0:T(8,128)(2,1)S(1)} %bitcast.89, f32[2,4,256,96,5]{2,3,4,1,0:T(8,128)} %copy-done, f32[2,4,5,96]{3,2,1,0:T(8,128)S(1)} %max.19, pred[2,96,256]{2,1,0:T(8,128)(4,1)S(1)} %copy-done.1, ...), kind=kOutput, calls=%fused_computation.7.clone.1 | convolution fusion | flops 256573440 | bytes 8468480 | tf_op jit(solution)/shard_map/while/body/eval_jaxpr/chgrn,cnhd->chgrd/dot_general | solution.py:42
  268.5 27.6 %all-gather.14.cloned.1.call-done = bf16[8,96,2560]{2,1,0:T(8,128)(2,1)} async-done(((bf16[2,96,2560]{2,1,0:T(8,128)(2,1)}), bf16[8,96,2560]{2,1,0:T(8,128)(2,1)}) %all-gather.14.cloned.1.call-update) | async-done | bytes 3932176 | tf_op jit(solution)/shard_map/all_gather | solution.py:135
  (131 shorter events, 35.4 us)
Async XLA Ops:
  6.5 63.1 %all-gather.6.cloned.1.call-start = ((), (), s32[]{:S(2)}) async-start(), calls=%async_computation | async-start | bytes 2162688 | tf_op jit(solution)/shard_map/all_gather | solution.py:90
  7.3 120.7 %all-gather.8.cloned.1.call-start = ((), (), s32[]{:S(2)}) async-start(), calls=%async_computation.1 | async-start | bytes 2162688 | tf_op jit(solution)/shard_map/all_gather | solution.py:91
  8.0 188.3 %all-gather.10.cloned.1.call-start = ((), (), s32[]{:S(2)}) async-start(), calls=%async_computation.2 | async-start | bytes 1769472 | tf_op jit(solution)/shard_map/all_gather | solution.py:119
  9.9 5.8 %copy-start.6 = (s32[8]{0:T(128)S(1)}, s32[8]{0:T(128)}, u32[]{:S(2)}) copy-start(s32[8]{0:T(128)} %param.18) | copy-start | bytes 100
  9.9 5.9 %copy-start.7 = (s32[8]{0:T(128)S(1)}, s32[8]{0:T(128)}, u32[]{:S(2)}) copy-start(s32[8]{0:T(128)} %param.17) | copy-start | bytes 100
  9.9 208.5 %all-gather.12.cloned.1.call-start = ((), (), s32[]{:S(2)}) async-start(), calls=%async_computation.3 | async-start | bytes 1769472 | tf_op jit(solution)/shard_map/all_gather | solution.py:120
  11.8 284.3 %all-gather.14.cloned.1.call-start = ((), (), s32[]{:S(2)}) async-start(), calls=%async_computation.4 | async-start | bytes 4915200 | tf_op jit(solution)/shard_map/all_gather | solution.py:135
  221.8 2.2 copy-start.2
  221.8 4.1 %copy-start.1 = (pred[2,96,256]{2,1,0:T(8,128)(4,1)S(1)}, pred[2,96,256]{2,1,0:T(8,128)(4,1)}, u32[]{:S(2)}) copy-start(pred[2,96,256]{2,1,0:T(8,128)(4,1)} %broadcast_and_fusion.2) | copy-start | bytes 147460 | tf_op jit(solution)/shard_map/while
  221.8 5.6 %copy-start.3 = (f32[2,4,5,96]{3,2,1,0:T(8,128)S(1)}, f32[2,4,5,96]{3,2,1,0:T(8,128)}, u32[]{:S(2)}) copy-start(f32[2,4,5,96]{3,2,1,0:T(8,128)} %get-tuple-element.705) | copy-start | bytes 46084 | tf_op jit(solution)/shard_map/while
  224.0 1.8 copy-start
  227.4 4.3 %copy-start.4 = (f32[2,4,5,96]{3,2,1,0:T(8,128)}, f32[2,4,5,96]{3,2,1,0:T(8,128)S(1)}, u32[]{:S(2)}) copy-start(f32[2,4,5,96]{3,2,1,0:T(8,128)S(1)} %get-tuple-element.719) | copy-start | bytes 46084 | tf_op jit(solution)/shard_map/while
  235.7 2.2 copy-start.2
  235.7 4.1 %copy-start.1 = (pred[2,96,256]{2,1,0:T(8,128)(4,1)S(1)}, pred[2,96,256]{2,1,0:T(8,128)(4,1)}, u32[]{:S(2)}) copy-start(pred[2,96,256]{2,1,0:T(8,128)(4,1)} %broadcast_and_fusion.2) | copy-start | bytes 147460 | tf_op jit(solution)/shard_map/while
  235.7 5.6 %copy-start.3 = (f32[2,4,5,96]{3,2,1,0:T(8,128)S(1)}, f32[2,4,5,96]{3,2,1,0:T(8,128)}, u32[]{:S(2)}) copy-start(f32[2,4,5,96]{3,2,1,0:T(8,128)} %get-tuple-element.705) | copy-start | bytes 46084 | tf_op jit(solution)/shard_map/while
  237.9 1.8 copy-start
  241.4 4.3 %copy-start.4 = (f32[2,4,5,96]{3,2,1,0:T(8,128)}, f32[2,4,5,96]{3,2,1,0:T(8,128)S(1)}, u32[]{:S(2)}) copy-start(f32[2,4,5,96]{3,2,1,0:T(8,128)S(1)} %get-tuple-element.719) | copy-start | bytes 46084 | tf_op jit(solution)/shard_map/while
  249.6 2.2 copy-start.2
  249.6 4.1 %copy-start.1 = (pred[2,96,256]{2,1,0:T(8,128)(4,1)S(1)}, pred[2,96,256]{2,1,0:T(8,128)(4,1)}, u32[]{:S(2)}) copy-start(pred[2,96,256]{2,1,0:T(8,128)(4,1)} %broadcast_and_fusion.2) | copy-start | bytes 147460 | tf_op jit(solution)/shard_map/while
  249.7 5.6 %copy-start.3 = (f32[2,4,5,96]{3,2,1,0:T(8,128)S(1)}, f32[2,4,5,96]{3,2,1,0:T(8,128)}, u32[]{:S(2)}) copy-start(f32[2,4,5,96]{3,2,1,0:T(8,128)} %get-tuple-element.705) | copy-start | bytes 46084 | tf_op jit(solution)/shard_map/while
  251.9 1.8 copy-start
  255.3 4.3 %copy-start.4 = (f32[2,4,5,96]{3,2,1,0:T(8,128)}, f32[2,4,5,96]{3,2,1,0:T(8,128)S(1)}, u32[]{:S(2)}) copy-start(f32[2,4,5,96]{3,2,1,0:T(8,128)S(1)} %get-tuple-element.719) | copy-start | bytes 46084 | tf_op jit(solution)/shard_map/while
  261.5 2.6 copy-start.5
Sparse Core Ops, SparseCore 0:
  10.3 59.2 all-gather.5
  72.6 55.3 all-gather.7
  130.2 43.0 all-gather.9
  175.3 43.0 all-gather.11
  264.3 31.7 all-gather.13
where the time goes:
time: 306 us; the launch traced here: 305 us
  waiting for transfers between devices  163 us (53%)
  matrix products  57.7 us (19%)
  local copies, waits for them, and re-layouts  36.7 us (12%)
  other arithmetic  29.6 us (10%)
  between operations  16.9 us (6%)
    all_gather x1, waiting for transfers between devices, body(): lax.all_gather(prompt_value_array, ('cand', 'seq'), axis=0, tiled=True)  58.4 us
    all_gather x1, waiting for transfers between devices, body(): lax.all_gather(prompt_key_array, ('cand', 'seq'), axis=0, tiled=True)  53.7 us
    all_gather x1, waiting for transfers between devices, body(): gathered = lax.all_gather(attended, 'cand', axis=0, tiled=True)  27.6 us
    dot_general x4, matrix products, attend_block(): jnp.einsum('chgrn,nhd->chgrd', weights, values_split, preferred_element_t...  23.1 us
    reduce_sum x7, other arithmetic, attend_block(): new_total = running_total * rescale + jnp.sum(exponent, axis=-1)  22.3 us
    all_gather x1, waiting for transfers between devices, body(): lax.all_gather(response_value_array, 'seq', axis=1, tiled=True)  22.1 us
    dot_general x4, matrix products, attend_block(): jnp.einsum('crhgd,nhd->chgrn', query_rows, keys_split, preferred_element_...  16.9 us
    dynamic_slice x14, local copies, waits for them, and re-layouts, one_block(): lax.dynamic_slice_in_dim(all_values, block_start, block_len, keys_axis)  13.3 us
  transfers between devices with their start and end apart: 5, of which 4 were waited for; matrix products, arithmetic and copies ran while one was open for 25% of the time, Pallas kernels for 0%

commit v1 on v0

--- a/solution.py
+++ b/solution.py
@@ -8,6 +8,19 @@
 KEY_VALUE_HEADS = 4
 HEAD_DIMENSION = 128
 lowest_score_value = -1e30
+
+
+def gather_around(value, axis, dim):
+    ways = lax.axis_size(axis)
+    up = [(d, (d + 1) % ways) for d in range(ways)]
+    down = [(d, (d - 1) % ways) for d in range(ways)]
+    earlier, later = ([value], [value])
+    for _ in range(ways // 2):
+        earlier.append(lax.ppermute(earlier[-1], axis, up))
+    for _ in range((ways - 1) // 2):
+        later.append(lax.ppermute(later[-1], axis, down))
+    line = jnp.concatenate([*earlier[::-1], *later[1:]], axis=dim)
+    return jnp.roll(line, (lax.axis_index(axis) - ways // 2) * value.shape[dim], axis=dim)
 
 
 def attend_block(running, query_rows, block_keys, block_values, allowed, shared):
@@ -117,7 +130,7 @@
     )
     pieces = (
         lax.all_gather(response_key_array, "seq", axis=1, tiled=True),
-        lax.all_gather(response_value_array, "seq", axis=1, tiled=True),
+        gather_around(response_value_array, "seq", 1),
     )
     key_pos = jnp.arange(pieces[0].shape[1], dtype=jnp.int32)
 

time: 306 us -> 275 us (0.90)
  waiting for transfers between devices: 163 us -> 121 us
  starting transfers between devices: 0.16 us -> 18.8 us
  matrix products: 57.7 us -> 52.5 us
    all_gather x1, waiting for transfers between devices: 53.7 us -> 6.49 us  [body(): lax.all_gather(prompt_key_array, ('cand', 'seq'), axis=0, tiled=True)]
    ppermute x0 -> x7, waiting for transfers between devices: none -> 26.4 us  [the longest x4 20.8 us: gather_around(): earlier.append(lax.ppermute(earlier[-1], axis, up))]
    all_gather x1 -> x0, waiting for transfers between devices: 22.1 us -> none  [body(): lax.all_gather(response_value_array, 'seq', axis=1, tiled=True)]
    ppermute x0 -> x7, starting transfers between devices: none -> 18.7 us  [the longest x3 10.7 us: gather_around(): later.append(lax.ppermute(later[-1], axis, down))]
    while x37 -> x7, local copies, waits for them, and re-layouts: 7.33 us -> 0.03 us
    concatenate x0 -> x1, local copies, waits for them, and re-layouts: none -> 6.14 us  [gather_around(): jnp.roll(line, (lax.axis_index(axis) - ways // 2) * value.shape[dim], axi...]
    dot_general x3, matrix products: 11.1 us -> 6.01 us  [attend_block(): jnp.einsum('chgrn,cnhd->chgrd', weights, values_split, preferred_element_...]
    dynamic_slice x7 -> x10, local copies, waits for them, and re-layouts: 2.48 us -> 6.71 us  [one_block(): lax.dynamic_slice_in_dim(all_keys, block_start, block_len, keys_axis)]
  transfers between devices with their start and end apart: 5 -> 11, of which waited for: 4 -> 8; matrix products, arithmetic and copies ran while one was open for 25% -> 31% of each run, Pallas kernels for 0% -> 0%
where the time goes in v1:
time: 275 us; the launch traced here: 273 us
  waiting for transfers between devices  121 us (44%)
  matrix products  52.5 us (19%)
  local copies, waits for them, and re-layouts  37.1 us (13%)
  other arithmetic  27 us (10%)
  starting transfers between devices  18.8 us (7%)
  between operations  16.9 us (6%)
    all_gather x1, waiting for transfers between devices, body(): lax.all_gather(prompt_value_array, ('cand', 'seq'), axis=0, tiled=True)  58.4 us
    all_gather x1, waiting for transfers between devices, body(): gathered = lax.all_gather(attended, 'cand', axis=0, tiled=True)  27.9 us
    dot_general x4, matrix products, attend_block(): jnp.einsum('chgrn,nhd->chgrd', weights, values_split, preferred_element_t...  23.1 us
    reduce_sum x7, other arithmetic, attend_block(): new_total = running_total * rescale + jnp.sum(exponent, axis=-1)  22.4 us
    ppermute x4, waiting for transfers between devices, gather_around(): earlier.append(lax.ppermute(earlier[-1], axis, up))  20.8 us
    dot_general x4, matrix products, attend_block(): jnp.einsum('crhgd,nhd->chgrn', query_rows, keys_split, preferred_element_...  16.9 us
    ppermute x3, starting transfers between devices, gather_around(): later.append(lax.ppermute(later[-1], axis, down))  10.7 us
    dynamic_slice x11, local copies, waits for them, and re-layouts, one_block(): lax.dynamic_slice_in_dim(all_values, block_start, block_len, keys_axis)  9.17 us
  transfers between devices with their start and end apart: 11, of which 8 were waited for; matrix products, arithmetic and copies ran while one was open for 31% of the time, Pallas kernels for 0%

profile of v1, /device:TPU:0, one launch (start us, length us, event | category | flops | bytes accessed | tf_op | source)
XLA Modules:
  0.0 273.4 jit_solution(17922067550043073710)
XLA Ops:
  9.2 3.0 %collective-permute-start = (bf16[2,96,512]{1,2,0:T(8,128)(2,1)S(1)}, bf16[2,96,512]{1,2,0:T(8,128)(2,1)S(1)}, u32[]{:S(2)}, u32[]{:S(2)}) collective-permute-start(bf16[2,96,512]{1,2,0:T(8,128)(2,1)S(1)} %copy.62), channel_id=1, source_target_pairs={{0,1},{1,2},{2,3},{3,4},{4,5},{5,6},{6,7},{7,0},{8,9},{9,10},{10,1... | collective-permute-start | bytes 589832 | tf_op jit(solution)/shard_map/ppermute | solution.py:19
  12.2 3.1 %collective-permute-start.4 = (bf16[2,96,512]{1,2,0:T(8,128)(2,1)S(1)}, bf16[2,96,512]{1,2,0:T(8,128)(2,1)S(1)}, u32[]{:S(2)}, u32[]{:S(2)}) collective-permute-start(bf16[2,96,512]{1,2,0:T(8,128)(2,1)S(1)} %copy.62), channel_id=1, source_target_pairs={{0,7},{1,0},{2,1},{3,2},{4,3},{5,4},{6,5},{7,6},{8,15},{9,8},{10,9... | collective-permute-start | bytes 589832 | tf_op jit(solution)/shard_map/ppermute | solution.py:21
  15.3 8.5 %collective-permute-done = bf16[2,96,512]{1,2,0:T(8,128)(2,1)S(1)} collective-permute-done((bf16[2,96,512]{1,2,0:T(8,128)(2,1)S(1)}, bf16[2,96,512]{1,2,0:T(8,128)(2,1)S(1)}, u32[]{:S(2)}, u32[]{:S(2)}) %collective-permute-start) | collective-permute-done | bytes 196640 | tf_op jit(solution)/shard_map/ppermute | solution.py:19
  23.8 2.5 collective-permute-start.1
  26.3 3.0 %collective-permute-start.5 = (bf16[2,96,512]{1,2,0:T(8,128)(2,1)S(1)}, bf16[2,96,512]{1,2,0:T(8,128)(2,1)}, u32[]{:S(2)}, u32[]{:S(2)}) collective-permute-start(bf16[2,96,512]{1,2,0:T(8,128)(2,1)S(1)} %collective-permute-done.4), channel_id=1, source_target_pairs={{0,7},{1,0},{2,1},{3,2},{4,3},{5,4},{6,5},{7,6},{8,15},{9,8},{10,9... | collective-permute-start | bytes 589832 | tf_op jit(solution)/shard_map/ppermute | solution.py:21
  29.4 7.5 %collective-permute-done.1 = bf16[2,96,512]{1,2,0:T(8,128)(2,1)S(1)} collective-permute-done((bf16[2,96,512]{1,2,0:T(8,128)(2,1)S(1)}, bf16[2,96,512]{1,2,0:T(8,128)(2,1)S(1)}, u32[]{:S(2)}, u32[]{:S(2)}) %collective-permute-start.1) | collective-permute-done | bytes 196640 | tf_op jit(solution)/shard_map/ppermute | solution.py:19
  36.9 2.5 collective-permute-start.2
  45.2 4.6 %collective-permute-start.6 = (bf16[2,96,512]{1,2,0:T(8,128)(2,1)}, bf16[2,96,512]{1,2,0:T(8,128)(2,1)S(1)}, u32[]{:S(2)}, u32[]{:S(2)}) collective-permute-start(bf16[2,96,512]{1,2,0:T(8,128)(2,1)} %collective-permute-done.5), channel_id=1, source_target_pairs={{0,7},{1,0},{2,1},{3,2},{4,3},{5,4},{6,5},{7,6},{8,15},{9,8},{10,9... | collective-permute-start | bytes 589832 | tf_op jit(solution)/shard_map/ppermute | solution.py:21
  50.0 5.6 %collective-permute-done.6 = bf16[2,96,512]{1,2,0:T(8,128)(2,1)S(1)} collective-permute-done((bf16[2,96,512]{1,2,0:T(8,128)(2,1)}, bf16[2,96,512]{1,2,0:T(8,128)(2,1)S(1)}, u32[]{:S(2)}, u32[]{:S(2)}) %collective-permute-start.6) | collective-permute-done | bytes 196640 | tf_op jit(solution)/shard_map/ppermute | solution.py:21
  55.6 4.6 %collective-permute-done.3 = bf16[2,96,512]{1,2,0:T(8,128)(2,1)S(1)} collective-permute-done((bf16[2,96,512]{1,2,0:T(8,128)(2,1)}, bf16[2,96,512]{1,2,0:T(8,128)(2,1)S(1)}, u32[]{:S(2)}, u32[]{:S(2)}) %collective-permute-start.3) | collective-permute-done | bytes 196640 | tf_op jit(solution)/shard_map/ppermute | solution.py:19
  60.2 6.1 %concatenate.6 = bf16[2,1536,512]{1,2,0:T(8,128)(2,1)} concatenate(bf16[2,96,512]{1,2,0:T(8,128)(2,1)S(1)} %collective-permute-done.3, bf16[2,96,512]{1,2,0:T(8,128)(2,1)} %collective-permute-done.2, bf16[2,96,512]{1,2,0:T(8,128)(2,1)S(1)} %collective-permute-done.1, bf16[2,96,512]{1,2,0:T(8,128)(2,1)S(1)} %collective-permute-done, bf16[2,96,512]{1,2,0:T(8,128)(2,1)S(1)} %copy.62, ...), dimensions={1} | concatenate | bytes 6291456 | tf_op jit(solution)/shard_map/jit(_roll_dynamic)/concatenate | solution.py:23
  66.3 3.4 %constant_dynamic-slice_fusion.6 = bf16[2,768,512]{1,2,0:T(8,128)(2,1)} fusion(bf16[2,1536,512]{1,2,0:T(8,128)(2,1)} %concatenate.6, s32[]{:T(128)S(6)} %select_n.71), kind=kLoop, calls=%fused_computation.50 | loop fusion | bytes 3145732 | tf_op jit(solution)/shard_map/jit(_roll_dynamic)/dynamic_slice | solution.py:23
  69.7 6.5 %all-gather.5.cloned.1.call-done = bf16[2048,512]{1,0:T(8,128)(2,1)} async-done(((bf16[64,512]{1,0:T(8,128)(2,1)}), bf16[2048,512]{1,0:T(8,128)(2,1)}) %all-gather.5.cloned.1.call-update) | async-done | bytes 2097168 | tf_op jit(solution)/shard_map/all_gather | solution.py:103
  76.2 58.4 %all-gather.7.cloned.1.call-done = bf16[2048,512]{1,0:T(8,128)(2,1)} async-done(((bf16[64,512]{1,0:T(8,128)(2,1)}), bf16[2048,512]{1,0:T(8,128)(2,1)}) %all-gather.7.cloned.1.call-update) | async-done | bytes 2097168 | tf_op jit(solution)/shard_map/all_gather | solution.py:104
  134.6 65.4 %while.37 = (s32[]{:T(128)}, f32[2,4,5,96]{3,2,0,1:T(8,128)S(1)}, f32[2,4,5,96]{3,2,0,1:T(8,128)S(1)}, f32[2,4,5,96,128]{4,3,2,0,1:T(8,128)}, s32[2048]{0:T(1024...) while((s32[]{:T(128)}, f32[2,4,5,96]{3,2,0,1:T(8,128)S(1)}, ...), condition=%wide.region_3.4_spmd.clone, body=%wide.region_0.3_spmd.clone.sunk | while | flops 1029754624 | bytes 34007244 | solution.py:78
  136.2 4.2 %fusion.60 = (f32[2,4,5,96]{3,2,0,1:T(8,128)S(1)}, f32[4,512,2,96,5]{1,3,4,2,0:T(8,128)}) fusion(pred[2,512]{1,0:T(4,128)(4,1)S(1)} %broadcast_compare_fusion.9, bf16[512,4,128,1,1]{0,2,4,3,1:T(8,128)(2,1)S(1)} %bitcast.88, bf16[2,96,4,5,128]{4,1,3,0,2:T(8,128)(2,1)S(1)} %get-tuple-element.677), kind=kOutput, calls=%fused_computation.26.clone.1 | convolution fusion | flops 509210880 | bytes 9388032 | tf_op jit(solution)/shard_map/while/body/eval_jaxpr/crhgd,nhd->chgrn/dot_general | solution.py:35
  140.5 4.5 %fusion.61 = f32[2,4,5,96]{3,2,0,1:T(8,128)S(1)} fusion(f32[4,512,2,96,5]{1,3,4,2,0:T(8,128)} %get-tuple-element.640, f32[2,4,5,96]{3,2,0,1:T(8,128)S(1)} %select_maximum_fusion.2, pred[2,512]{1,0:T(4,128)(4,1)S(1)} %broadcast_compare_fusion.9), kind=kLoop, calls=%fused_computation.25.clone.1 | loop fusion | flops 7860480 | bytes 7896064 | tf_op jit(solution)/shard_map/while/body/eval_jaxpr/reduce_sum | solution.py:49
  145.2 5.4 %bitcast_add_fusion.2 = f32[2,4,5,96,128]{4,3,2,0,1:T(8,128)} fusion(f32[2,4,5,96,128]{4,3,2,0,1:T(8,128)} %get-tuple-element.660, bf16[512,4,128,1,1]{0,2,4,3,1:T(8,128)(2,1)S(1)} %bitcast.91, f32[4,512,2,96,5]{1,3,4,2,0:T(8,128)} %get-tuple-element.640, f32[2,4,5,96]{3,2,0,1:T(8,128)S(1)} %select_maximum_fusion.2, ...), kind=kOutput, calls=%fused_computation.32.clone.1 | convolution fusion | flops 512655360 | bytes 12352513 | tf_op jit(solution)/shard_map/while/body/eval_jaxpr/chgrn,nhd->chgrd/dot_general | solution.py:51
  152.3 4.2 %fusion.60 = (f32[2,4,5,96]{3,2,0,1:T(8,128)S(1)}, f32[4,512,2,96,5]{1,3,4,2,0:T(8,128)}) fusion(pred[2,512]{1,0:T(4,128)(4,1)S(1)} %broadcast_compare_fusion.9, bf16[512,4,128,1,1]{0,2,4,3,1:T(8,128)(2,1)S(1)} %bitcast.88, bf16[2,96,4,5,128]{4,1,3,0,2:T(8,128)(2,1)S(1)} %get-tuple-element.677), kind=kOutput, calls=%fused_computation.26.clone.1 | convolution fusion | flops 509210880 | bytes 9388032 | tf_op jit(solution)/shard_map/while/body/eval_jaxpr/crhgd,nhd->chgrn/dot_general | solution.py:35
  156.5 4.4 %fusion.61 = f32[2,4,5,96]{3,2,0,1:T(8,128)S(1)} fusion(f32[4,512,2,96,5]{1,3,4,2,0:T(8,128)} %get-tuple-element.640, f32[2,4,5,96]{3,2,0,1:T(8,128)S(1)} %select_maximum_fusion.2, pred[2,512]{1,0:T(4,128)(4,1)S(1)} %broadcast_compare_fusion.9), kind=kLoop, calls=%fused_computation.25.clone.1 | loop fusion | flops 7860480 | bytes 7896064 | tf_op jit(solution)/shard_map/while/body/eval_jaxpr/reduce_sum | solution.py:49
  161.2 6.0 %bitcast_add_fusion.2 = f32[2,4,5,96,128]{4,3,2,0,1:T(8,128)} fusion(f32[2,4,5,96,128]{4,3,2,0,1:T(8,128)} %get-tuple-element.660, bf16[512,4,128,1,1]{0,2,4,3,1:T(8,128)(2,1)S(1)} %bitcast.91, f32[4,512,2,96,5]{1,3,4,2,0:T(8,128)} %get-tuple-element.640, f32[2,4,5,96]{3,2,0,1:T(8,128)S(1)} %select_maximum_fusion.2, ...), kind=kOutput, calls=%fused_computation.32.clone.1 | convolution fusion | flops 512655360 | bytes 12352513 | tf_op jit(solution)/shard_map/while/body/eval_jaxpr/chgrn,nhd->chgrd/dot_general | solution.py:51
  168.8 4.2 %fusion.60 = (f32[2,4,5,96]{3,2,0,1:T(8,128)S(1)}, f32[4,512,2,96,5]{1,3,4,2,0:T(8,128)}) fusion(pred[2,512]{1,0:T(4,128)(4,1)S(1)} %broadcast_compare_fusion.9, bf16[512,4,128,1,1]{0,2,4,3,1:T(8,128)(2,1)S(1)} %bitcast.88, bf16[2,96,4,5,128]{4,1,3,0,2:T(8,128)(2,1)S(1)} %get-tuple-element.677), kind=kOutput, calls=%fused_computation.26.clone.1 | convolution fusion | flops 509210880 | bytes 9388032 | tf_op jit(solution)/shard_map/while/body/eval_jaxpr/crhgd,nhd->chgrn/dot_general | solution.py:35
  173.0 4.4 %fusion.61 = f32[2,4,5,96]{3,2,0,1:T(8,128)S(1)} fusion(f32[4,512,2,96,5]{1,3,4,2,0:T(8,128)} %get-tuple-element.640, f32[2,4,5,96]{3,2,0,1:T(8,128)S(1)} %select_maximum_fusion.2, pred[2,512]{1,0:T(4,128)(4,1)S(1)} %broadcast_compare_fusion.9), kind=kLoop, calls=%fused_computation.25.clone.1 | loop fusion | flops 7860480 | bytes 7896064 | tf_op jit(solution)/shard_map/while/body/eval_jaxpr/reduce_sum | solution.py:49
  177.7 5.9 %bitcast_add_fusion.2 = f32[2,4,5,96,128]{4,3,2,0,1:T(8,128)} fusion(f32[2,4,5,96,128]{4,3,2,0,1:T(8,128)} %get-tuple-element.660, bf16[512,4,128,1,1]{0,2,4,3,1:T(8,128)(2,1)S(1)} %bitcast.91, f32[4,512,2,96,5]{1,3,4,2,0:T(8,128)} %get-tuple-element.640, f32[2,4,5,96]{3,2,0,1:T(8,128)S(1)} %select_maximum_fusion.2, ...), kind=kOutput, calls=%fused_computation.32.clone.1 | convolution fusion | flops 512655360 | bytes 12352513 | tf_op jit(solution)/shard_map/while/body/eval_jaxpr/chgrn,nhd->chgrd/dot_general | solution.py:51
  185.2 4.2 %fusion.60 = (f32[2,4,5,96]{3,2,0,1:T(8,128)S(1)}, f32[4,512,2,96,5]{1,3,4,2,0:T(8,128)}) fusion(pred[2,512]{1,0:T(4,128)(4,1)S(1)} %broadcast_compare_fusion.9, bf16[512,4,128,1,1]{0,2,4,3,1:T(8,128)(2,1)S(1)} %bitcast.88, bf16[2,96,4,5,128]{4,1,3,0,2:T(8,128)(2,1)S(1)} %get-tuple-element.677), kind=kOutput, calls=%fused_computation.26.clone.1 | convolution fusion | flops 509210880 | bytes 9388032 | tf_op jit(solution)/shard_map/while/body/eval_jaxpr/crhgd,nhd->chgrn/dot_general | solution.py:35
  189.5 4.4 %fusion.61 = f32[2,4,5,96]{3,2,0,1:T(8,128)S(1)} fusion(f32[4,512,2,96,5]{1,3,4,2,0:T(8,128)} %get-tuple-element.640, f32[2,4,5,96]{3,2,0,1:T(8,128)S(1)} %select_maximum_fusion.2, pred[2,512]{1,0:T(4,128)(4,1)S(1)} %broadcast_compare_fusion.9), kind=kLoop, calls=%fused_computation.25.clone.1 | loop fusion | flops 7860480 | bytes 7896064 | tf_op jit(solution)/shard_map/while/body/eval_jaxpr/reduce_sum | solution.py:49
  194.1 5.9 %bitcast_add_fusion.2 = f32[2,4,5,96,128]{4,3,2,0,1:T(8,128)} fusion(f32[2,4,5,96,128]{4,3,2,0,1:T(8,128)} %get-tuple-element.660, bf16[512,4,128,1,1]{0,2,4,3,1:T(8,128)(2,1)S(1)} %bitcast.91, f32[4,512,2,96,5]{1,3,4,2,0:T(8,128)} %get-tuple-element.640, f32[2,4,5,96]{3,2,0,1:T(8,128)S(1)} %select_maximum_fusion.2, ...), kind=kOutput, calls=%fused_computation.32.clone.1 | convolution fusion | flops 512655360 | bytes 12352513 | tf_op jit(solution)/shard_map/while/body/eval_jaxpr/chgrn,nhd->chgrd/dot_general | solution.py:51
  201.8 27.5 %while.36 = (s32[]{:T(128)}, f32[2,4,5,96]{3,2,1,0:T(8,128)S(1)}, f32[2,4,5,96]{3,2,1,0:T(8,128)S(1)}, f32[2,4,5,96,128]{4,3,2,1,0:T(8,128)S(1)}, s32[768]{0:T(1...) while((s32[]{:T(128)}, f32[2,4,5,96]{3,2,1,0:T(8,128)S(1)}, ...), condition=%wide.region_7.8_spmd.clone, body=%wide.region_4.7_spmd.clone.sunk | while | flops 515194976 | bytes 21403604 | solution.py:78
  204.0 2.2 fusion.54
  213.2 2.2 fusion.54
  222.3 2.2 fusion.54
  236.7 27.9 %all-gather.11.cloned.1.call-done = bf16[8,96,2560]{2,1,0:T(8,128)(2,1)} async-done(((bf16[2,96,2560]{2,1,0:T(8,128)(2,1)}), bf16[8,96,2560]{2,1,0:T(8,128)(2,1)}) %all-gather.11.cloned.1.call-update) | async-done | bytes 3932176 | tf_op jit(solution)/shard_map/all_gather | solution.py:148
  (114 shorter events, 44.6 us)
Async XLA Ops:
  6.5 69.7 %all-gather.5.cloned.1.call-start = ((), (), s32[]{:S(2)}) async-start(), calls=%async_computation | async-start | bytes 2162688 | tf_op jit(solution)/shard_map/all_gather | solution.py:103
  7.3 127.3 %all-gather.7.cloned.1.call-start = ((), (), s32[]{:S(2)}) async-start(), calls=%async_computation.1 | async-start | bytes 2162688 | tf_op jit(solution)/shard_map/all_gather | solution.py:104
  8.0 37.0 %copy-start.1 = (s32[8]{0:T(128)S(1)}, s32[8]{0:T(128)}, u32[]{:S(2)}) copy-start(s32[8]{0:T(128)} %param.18) | copy-start | bytes 100
  8.0 37.1 %copy-start.2 = (s32[8]{0:T(128)S(1)}, s32[8]{0:T(128)}, u32[]{:S(2)}) copy-start(s32[8]{0:T(128)} %param.17) | copy-start | bytes 100
  8.0 193.7 %all-gather.9.cloned.1.call-start = ((), (), s32[]{:S(2)}) async-start(), calls=%async_computation.2 | async-start | bytes 1769472 | tf_op jit(solution)/shard_map/all_gather | solution.py:132
  9.2 14.7 %collective-permute-start = (bf16[2,96,512]{1,2,0:T(8,128)(2,1)S(1)}, bf16[2,96,512]{1,2,0:T(8,128)(2,1)S(1)}, u32[]{:S(2)}, u32[]{:S(2)}) collective-permute-start(bf16[2,96,512]{1,2,0:T(8,128)(2,1)S(1)} %copy.62), channel_id=1, source_target_pairs={{0,1},{1,2},{2,3},{3,4},{4,5},{5,6},{6,7},{7,0},{8,9},{9,10},{10,1... | collective-permute-start | bytes 589832 | tf_op jit(solution)/shard_map/ppermute | solution.py:19
  12.2 14.1 %collective-permute-start.4 = (bf16[2,96,512]{1,2,0:T(8,128)(2,1)S(1)}, bf16[2,96,512]{1,2,0:T(8,128)(2,1)S(1)}, u32[]{:S(2)}, u32[]{:S(2)}) collective-permute-start(bf16[2,96,512]{1,2,0:T(8,128)(2,1)S(1)} %copy.62), channel_id=1, source_target_pairs={{0,7},{1,0},{2,1},{3,2},{4,3},{5,4},{6,5},{7,6},{8,15},{9,8},{10,9... | collective-permute-start | bytes 589832 | tf_op jit(solution)/shard_map/ppermute | solution.py:21
  23.8 13.0 %collective-permute-start.1 = (bf16[2,96,512]{1,2,0:T(8,128)(2,1)S(1)}, bf16[2,96,512]{1,2,0:T(8,128)(2,1)S(1)}, u32[]{:S(2)}, u32[]{:S(2)}) collective-permute-start(bf16[2,96,512]{1,2,0:T(8,128)(2,1)S(1)} %collective-permute-done), channel_id=1, source_target_pairs={{0,1},{1,2},{2,3},{3,4},{4,5},{5,6},{6,7},{7,0},{8,9},{9,10},{10,1... | collective-permute-start | bytes 589832 | tf_op jit(solution)/shard_map/ppermute | solution.py:19
  26.3 18.9 %collective-permute-start.5 = (bf16[2,96,512]{1,2,0:T(8,128)(2,1)S(1)}, bf16[2,96,512]{1,2,0:T(8,128)(2,1)}, u32[]{:S(2)}, u32[]{:S(2)}) collective-permute-start(bf16[2,96,512]{1,2,0:T(8,128)(2,1)S(1)} %collective-permute-done.4), channel_id=1, source_target_pairs={{0,7},{1,0},{2,1},{3,2},{4,3},{5,4},{6,5},{7,6},{8,15},{9,8},{10,9... | collective-permute-start | bytes 589832 | tf_op jit(solution)/shard_map/ppermute | solution.py:21
  36.9 13.0 %collective-permute-start.2 = (bf16[2,96,512]{1,2,0:T(8,128)(2,1)S(1)}, bf16[2,96,512]{1,2,0:T(8,128)(2,1)}, u32[]{:S(2)}, u32[]{:S(2)}) collective-permute-start(bf16[2,96,512]{1,2,0:T(8,128)(2,1)S(1)} %collective-permute-done.1), channel_id=1, source_target_pairs={{0,1},{1,2},{2,3},{3,4},{4,5},{5,6},{6,7},{7,0},{8,9},{9,10},{10,1... | collective-permute-start | bytes 589832 | tf_op jit(solution)/shard_map/ppermute | solution.py:19
  41.2 223.4 %all-gather.11.cloned.1.call-start = ((), (), s32[]{:S(2)}) async-start(), calls=%async_computation.3 | async-start | bytes 4915200 | tf_op jit(solution)/shard_map/all_gather | solution.py:148
  45.2 10.4 %collective-permute-start.6 = (bf16[2,96,512]{1,2,0:T(8,128)(2,1)}, bf16[2,96,512]{1,2,0:T(8,128)(2,1)S(1)}, u32[]{:S(2)}, u32[]{:S(2)}) collective-permute-start(bf16[2,96,512]{1,2,0:T(8,128)(2,1)} %collective-permute-done.5), channel_id=1, source_target_pairs={{0,7},{1,0},{2,1},{3,2},{4,3},{5,4},{6,5},{7,6},{8,15},{9,8},{10,9... | collective-permute-start | bytes 589832 | tf_op jit(solution)/shard_map/ppermute | solution.py:21
  49.8 10.4 %collective-permute-start.3 = (bf16[2,96,512]{1,2,0:T(8,128)(2,1)}, bf16[2,96,512]{1,2,0:T(8,128)(2,1)S(1)}, u32[]{:S(2)}, u32[]{:S(2)}) collective-permute-start(bf16[2,96,512]{1,2,0:T(8,128)(2,1)} %collective-permute-done.2), channel_id=1, source_target_pairs={{0,1},{1,2},{2,3},{3,4},{4,5},{5,6},{6,7},{7,0},{8,9},{9,10},{10,1... | collective-permute-start | bytes 589832 | tf_op jit(solution)/shard_map/ppermute | solution.py:19
  229.8 2.6 copy-start
Sparse Core Ops, SparseCore 0:
  10.3 65.8 all-gather.4
  79.2 55.3 all-gather.6
  136.8 43.0 all-gather.8
  232.5 31.9 all-gather.10
